TPU v7x, 256 devices: a whole 4x4x8 slice. The times are simulated.
256 devices in a mesh: ctx: 32 (over z, x), head: 4 (over y_hi, core), side: 2 (over y_lo).
Axes of the slice: x: 4, y: 4 (y_hi: 2, y_lo: 2; y = y_hi * 2 + y_lo), z: 8, core: 2. Of those that a mesh axis runs over, the one named last changes fastest.
Arguments:
- prefill_query: bfloat16 [8192, 64, 128], P('ctx', ('head', 'side')), may hold values from -6 to 6
- prefill_keys: bfloat16 [8192, 8, 128], P('ctx', ('head', 'side')), may hold values from -6 to 6
- prefill_values: bfloat16 [8192, 8, 128], P('ctx', ('head', 'side')), may hold values from -6 to 6
- token_pos: int32 [8192], P('ctx'), may hold values from 0 to 8191, as said below
- scale_exp: int32 [1024, 8, 2], P('ctx', ('head', 'side')), may hold values from -7 to -5
- page_owner: int32 [1024], P('ctx'), may hold values from 0 to 31, as said below
- draft_query: bfloat16 [256, 64, 128], P(None, ('head', 'side')), may hold values from -6 to 6
- draft_keys: bfloat16 [256, 8, 128], P('side', 'head'), may hold values from -6 to 6
- draft_values: bfloat16 [256, 8, 128], P('side', 'head'), may hold values from -6 to 6
- parents: int32 [256], replicated, may hold values from 0 to 254, as said below
Outputs:
- prefill_out: bfloat16 [8192, 64, 128], P('ctx', ('head', 'side'))
- cache_keys: bfloat16 [8192, 8, 128], P('ctx', ('head', 'side'))
- cache_values: bfloat16 [8192, 8, 128], P('ctx', ('head', 'side'))
- verify_out: bfloat16 [256, 64, 128], P('ctx', ('head', 'side'))
Inputs may be any that keep to these rules, and one draw needn't show every extreme that they name: `token_pos`: a permutation of 0 to 8191; the rows of shard c of ctx hold the runs a and 2 * 32 - 1 - a of 128 consecutive positions, in order, with a different a for each shard. `page_owner`: the 1024 // 32 entries of one ctx shard are a permutation of 0 to 32 - 1. parents[0] = 0, and parents[r] < r for r >= 1.
All inputs are finite; a program needn't handle non-finite values.
Results may differ from a plain program's by a relative error of at most 0.0049.
Values may be sent and summed in bfloat16 or wider, within the bound.
No kernel may reach another device: no remote copies, remote signals or barrier semaphores. Data moves between devices by JAX's collectives and lax.ppermute only.
A program may use at most 64 MiB of HBM per device.

v0:
```python
import math
import jax
import jax.numpy as jnp
import numpy as np
from jax import lax
from jax.sharding import Mesh
from jax.sharding import PartitionSpec as P

CTX = ("ctx_0", "ctx_1")
NEG_FILL = -1e30
FP_LIMIT = 448.0
LOG_TWO_E = 1.4426950408889634


def side_by_side(arrays, axis, dim, along):
    widths = [a.shape[along] for a in arrays]
    both = jnp.concatenate(arrays, axis=along)
    whole = lax.all_gather(both, axis, axis=dim, tiled=True)
    return tuple(jnp.split(whole, [sum(widths[:k]) for k in range(1, len(widths))], axis=along))


def sent_together(arrays, axis, split_dim, concat_dim, along):
    columns = [a.reshape(*a.shape[:along], -1) for a in arrays]
    both = jnp.concatenate(columns, axis=along)
    whole, at, outs = (
        lax.all_to_all(both, axis, split_axis=split_dim, concat_axis=concat_dim, tiled=True),
        0,
        [],
    )
    for a, column in zip(arrays, columns):
        section = whole[..., at : at + column.shape[along]]
        outs.append(section.reshape(*section.shape[:along], *a.shape[along:]))
        at += column.shape[along]
    return tuple(outs)


def sent_together_2(arrays, axis, split_dim, concat_dim, along):
    ends, at = ([], 0)
    for a in arrays[:-1]:
        at += a.shape[along]
        ends.append(at)
    both = jnp.concatenate(arrays, axis=along)
    return tuple(
        jnp.split(
            lax.all_to_all(both, axis, split_axis=split_dim, concat_axis=concat_dim, tiled=True),
            ends,
            axis=along,
        )
    )


def sent_to_all(array, axis):
    devices = lax.axis_size(axis)
    return lax.all_to_all(
        jnp.broadcast_to(array[None], (devices, *array.shape)), axis, 0, 0, tiled=True
    )


def taken_together(array, axis):
    everything = sent_to_all(array, axis)
    return jnp.max(everything, axis=0)


def summed_rows(array, axes, dim):
    if not axes:
        return array
    nearer = lax.psum_scatter(array, axes[0], scatter_dimension=dim, tiled=True)
    return summed_rows(nearer, axes[1:], dim)


def power_two(exponent):
    levels = jnp.arange(-7, -4, dtype=jnp.int32)
    table = jnp.asarray(np.array([2.0**level for level in range(-7, -4)], np.float32))
    return jnp.sum(jnp.where(exponent[..., None] == levels, table, jnp.float32(0.0)), axis=-1)


def ancestors(parent_rows):
    row_total = parent_rows.shape[0]
    row_index = jnp.arange(row_total, dtype=jnp.int32)
    linked = (
        (parent_rows[:, None] == row_index[None, :]) | (row_index[:, None] == row_index[None, :])
    ).astype(jnp.float32)
    for _ in range(row_total.bit_length()):
        linked = jnp.minimum(
            jnp.dot(linked, linked, precision=lax.Precision.HIGHEST), jnp.float32(1.0)
        )
    return linked > 0.5


def online_step(running, scores, allowed, value_block):
    old_top, old_mass, old_numer = running
    block_top = jnp.ceil(LOG_TWO_E * jnp.max(jnp.where(allowed, scores, NEG_FILL), axis=1))
    new_top = jnp.maximum(old_top, block_top)
    weights = jnp.where(allowed, jnp.exp2(LOG_TWO_E * scores - new_top[:, None]), jnp.float32(0.0))
    factor = jnp.exp2(old_top - new_top)
    new_mass = old_mass * factor + jnp.sum(weights, axis=1)
    new_numer = old_numer * factor[:, None] + jnp.dot(
        weights.astype(jnp.bfloat16), value_block, preferred_element_type=jnp.float32
    )
    return (new_top, new_mass, new_numer)


def body(
    prefill_query,
    prefill_keys,
    prefill_values,
    token_pos,
    scale_exp,
    page_owner,
    draft_query,
    draft_keys,
    draft_values,
    parents,
):
    tok_rows, groups, width = prefill_query.shape
    scale_factor = width ** (-0.5)
    shard_total = lax.axis_size(CTX)
    page_rows = tok_rows // shard_total
    my_index = lax.axis_index(CTX)
    query_rows = prefill_query.reshape(tok_rows * groups, width)
    query_places = jnp.repeat(token_pos, groups)
    local_keys = prefill_keys.reshape(tok_rows, width)
    local_values = prefill_values.reshape(tok_rows, width)
    page_scales = power_two(scale_exp.reshape(shard_total, 2))
    start_state = (
        jnp.full((tok_rows * groups,), NEG_FILL, jnp.float32),
        jnp.zeros((tok_rows * groups,), jnp.float32),
        jnp.zeros((tok_rows * groups, width), jnp.float32),
    )

    def attend(running, key_block, value_block, place_block):
        scores = scale_factor * jnp.einsum(
            "qd,kd->qk", query_rows, key_block, preferred_element_type=jnp.float32
        )
        allowed = query_places[:, None] >= place_block[None, :]
        return online_step(running, scores, allowed, value_block)

    running = start_state
    key_piece, value_piece, place_piece = (
        *side_by_side((local_keys, local_values), CTX, 0, 1),
        lax.all_gather(token_pos, CTX, axis=0, tiled=True),
    )
    row_count = key_piece.shape[0]
    block_rows = math.gcd(row_count, 512)
    block_total = row_count // block_rows

    def inner_rows(carry_in, item):
        return (attend(carry_in, item[0], item[1], item[2]), None)

    running, _ = lax.scan(
        inner_rows,
        running,
        (
            key_piece.reshape(block_total, block_rows, width),
            value_piece.reshape(block_total, block_rows, width),
            place_piece.reshape(block_total, block_rows),
        ),
    )
    paged_keys = local_keys.reshape(shard_total, page_rows, width).astype(jnp.float32)
    paged_values = local_values.reshape(shard_total, page_rows, width).astype(jnp.float32)
    scaled_keys = jnp.clip(paged_keys / page_scales[:, 0, None, None], -FP_LIMIT, FP_LIMIT).astype(
        jnp.bfloat16
    )
    scaled_values = jnp.clip(
        paged_values / page_scales[:, 1, None, None], -FP_LIMIT, FP_LIMIT
    ).astype(jnp.bfloat16)
    slot_index = jnp.arange(shard_total, dtype=jnp.int32)
    inverse = jnp.sum(
        jnp.where(page_owner[None, :] == slot_index[:, None], slot_index[None, :], 0), axis=1
    )
    got_keys, got_values, got_scales = sent_together(
        (
            jnp.take(scaled_keys, inverse, axis=0),
            jnp.take(scaled_values, inverse, axis=0),
            jnp.take(page_scales, inverse, axis=0).astype(jnp.bfloat16),
        ),
        CTX,
        0,
        0,
        1,
    )
    scale_back = got_scales.astype(jnp.float32)
    cache_keys = (
        (got_keys.astype(jnp.float32) * scale_back[:, 0, None, None])
        .astype(jnp.bfloat16)
        .reshape(tok_rows, width)
    )
    cache_values = (
        (got_values.astype(jnp.float32) * scale_back[:, 1, None, None])
        .astype(jnp.bfloat16)
        .reshape(tok_rows, width)
    )
    prefill_out = (
        (running[2] / running[1][:, None]).astype(jnp.bfloat16).reshape(tok_rows, groups, width)
    )
    tree_keys, tree_values = sent_together_2((draft_keys, draft_values), "side", 1, 0, 2)
    row_total = draft_query.shape[0]
    tree_keys = tree_keys.reshape(row_total, width)
    tree_values = tree_values.reshape(row_total, width)
    draft_rows = draft_query.reshape(row_total * groups, width)
    cache_scores = scale_factor * jnp.einsum(
        "qd,kd->qk", draft_rows, cache_keys, preferred_element_type=jnp.float32
    )
    cache_top = jnp.ceil(LOG_TWO_E * jnp.max(cache_scores, axis=1))
    tree_mask = jnp.repeat(ancestors(parents), groups, axis=0)
    tree_scores = scale_factor * jnp.einsum(
        "qd,kd->qk", draft_rows, tree_keys, preferred_element_type=jnp.float32
    )
    tree_top = jnp.ceil(LOG_TWO_E * jnp.max(jnp.where(tree_mask, tree_scores, NEG_FILL), axis=1))
    tree_weights = jnp.where(
        tree_mask, jnp.exp2(LOG_TWO_E * tree_scores - tree_top[:, None]), jnp.float32(0.0)
    )
    tree_mass = jnp.sum(tree_weights, axis=1)
    tree_numer = jnp.dot(
        tree_weights.astype(jnp.bfloat16), tree_values, preferred_element_type=jnp.float32
    )
    share_rows = row_total // shard_total

    def own_rows(array):
        return lax.dynamic_slice_in_dim(array, my_index * share_rows, share_rows, 0)

    global_top = taken_together(cache_top, CTX)
    cache_weights = jnp.exp2(LOG_TWO_E * cache_scores - global_top[:, None])
    cache_mass = jnp.sum(cache_weights, axis=1).reshape(row_total, groups)
    cache_numer = jnp.dot(
        cache_weights.astype(jnp.bfloat16), cache_values, preferred_element_type=jnp.float32
    ).reshape(row_total, groups, width)
    far_mass, far_numer = (summed_rows(cache_mass, CTX, 0), summed_rows(cache_numer, CTX, 0))
    far_top = own_rows(global_top.reshape(row_total, groups))
    near_top = own_rows(tree_top.reshape(row_total, groups))
    near_mass = own_rows(tree_mass.reshape(row_total, groups))
    near_numer = own_rows(tree_numer.reshape(row_total, groups, width))
    joint_top = jnp.maximum(far_top, near_top)
    far_factor = jnp.exp2(far_top - joint_top)
    near_factor = jnp.exp2(near_top - joint_top)
    numer_total = far_numer * far_factor[..., None] + near_numer * near_factor[..., None]
    mass_total = far_mass * far_factor + near_mass * near_factor
    verify_out = (numer_total / mass_total[..., None]).astype(jnp.bfloat16)
    return (
        prefill_out,
        cache_keys.reshape(tok_rows, 1, width),
        cache_values.reshape(tok_rows, 1, width),
        verify_out,
    )


def solution(mesh):
    finer = Mesh(
        mesh.devices.reshape(8, 4, mesh.shape["head"], mesh.shape["side"]),
        ("ctx_0", "ctx_1", "head", "side"),
    )
    in_specs = (
        P(CTX, ("head", "side"), None),
        P(CTX, ("head", "side"), None),
        P(CTX, ("head", "side"), None),
        P(CTX),
        P(CTX, ("head", "side"), None),
        P(CTX),
        P(None, ("head", "side"), None),
        P("side", "head", None),
        P("side", "head", None),
        P(),
    )
    out_specs = (
        P(CTX, ("head", "side"), None),
        P(CTX, ("head", "side"), None),
        P(CTX, ("head", "side"), None),
        P(CTX, ("head", "side"), None),
    )
    return jax.shard_map(body, mesh=finer, in_specs=in_specs, out_specs=out_specs, check_vma=False)
```

profile of v0, /device:TPU:8, one launch (start us, length us, event | category | flops | bytes accessed | tf_op | source)
XLA Modules:
  0.0 365.7 jit_solution(1240601794977269774)
XLA Ops:
  14.2 21.9 %all_to_all.36 = bf16[32,2,1025]{2,1,0:T(2,128)(2,1)S(1)} all-to-all(bf16[32,2,1025]{2,1,0:T(2,128)(2,1)S(1)} %reshape.283), channel_id=1, replica_groups=mesh['ctx_0'=8,'ctx_1'=4,'head'=4,'side'=2] {'ctx_0','ctx_1'}, dimensions={0} | all-to-all | bytes 262400 | tf_op jit(solution)/shard_map/all_to_all | solution.py:26
  37.9 3.9 %all-to-all-start.1 = ((f32[32,1,2048]{2,1,0:T(1,128)}), f32[32,1,2048]{2,1,0:T(1,128)S(1)}, u32[]{:S(2)}, u32[]{:S(2)}) async-start(f32[32,1,2048]{2,1,0:T(1,128)} %broadcast_in_dim.109), calls=%async_computation.1 | async-start | bytes 524288 | tf_op jit(solution)/shard_map/all_to_all | solution.py:54
  41.9 11.8 %all-to-all-done.1 = f32[32,1,2048]{2,1,0:T(1,128)S(1)} async-done(((f32[32,1,2048]{2,1,0:T(1,128)}), f32[32,1,2048]{2,1,0:T(1,128)S(1)}, u32[]{:S(2)}, u32[]{:S(2)}) %all-to-all-start.1) | async-done | bytes 262176 | tf_op jit(solution)/shard_map/all_to_all | solution.py:54
  59.2 33.4 %reduce-scatter.4.cloned.1.call-done = f32[32,8,128]{2,0,1:T(8,128)} async-done(((f32[256,8,128]{2,0,1:T(8,128)}), f32[32,8,128]{2,0,1:T(8,128)}) %reduce-scatter.4.cloned.1.call-update) | async-done | bytes 131088 | tf_op jit(solution)/shard_map/reduce_scatter | solution.py:67
  94.2 3.9 %all-to-all-start.2 = ((bf16[128,2,256]{2,0,1:T(8,128)(2,1)}), bf16[128,2,256]{2,0,1:T(8,128)(2,1)S(1)}, u32[]{:S(2)}, u32[]{:S(2)}) async-start(bf16[128,2,256]{2,0,1:T(8,128)(2,1)} %pad_maximum_fusion.1), calls=%async_computation.4 | async-start | bytes 262144 | tf_op jit(solution)/shard_map/all_to_all | solution.py:45
  101.8 42.4 %all-gather = s32[32,1,256]{2,1,0:T(1,128)S(1)} all-gather(s32[1,1,256]{2,1,0:T(1,128)S(1)} %bitcast.145), channel_id=1, replica_groups=mesh['ctx_0'=8,'ctx_1'=4,'head'=4,'side'=2] {'ctx_0','ctx_1'}, dimensions={0}, use_global_device_ids=true | all-gather | bytes 33792 | tf_op jit(solution)/shard_map/all_gather | solution.py:141
  153.2 16.3 %all-reduce = f32[32,8]{1,0:T(8,128)S(1)} all-reduce(f32[32,8]{1,0:T(8,128)} %reduce-scatter.8.cloned.1.call-done), channel_id=5, replica_groups=mesh['ctx_0'=8,'ctx_1'=4,'head'=4,'side'=2] {'ctx_1'}, use_global_device_ids=true, to_apply=%region_13.15.clone | all-reduce | flops 256 | bytes 2048
  171.9 5.0 %all-gather.3.cloned.1.call-done = bf16[8192,256]{1,0:T(8,128)(2,1)} async-done(((bf16[256,256]{1,0:T(8,128)(2,1)}), bf16[8192,256]{1,0:T(8,128)(2,1)}) %all-gather.3.cloned.1.call-update) | async-done | bytes 4194320 | tf_op jit(solution)/shard_map/all_gather | solution.py:18
  176.9 3.8 %fusion.54 = (bf16[8192,128]{1,0:T(8,128)(2,1)S(1)}, bf16[8192,128]{1,0:T(8,128)(2,1)}) fusion(bf16[8192,256]{1,0:T(8,128)(2,1)} %all-gather.3.cloned.1.call-done), kind=kLoop, calls=%fused_computation.116 | loop fusion | bytes 8388608 | tf_op jit(solution)/shard_map/split | solution.py:19
  180.7 175.6 %while.17 = (s32[]{:T(128)}, f32[2048]{0:T(1024)S(1)}, f32[2048]{0:T(1024)S(1)}, f32[2048,128]{1,0:T(8,128)}, s32[16,512]{1,0:T(8,128)S(1)}, /*index=5*/bf16[16,...) while((s32[]{:T(128)}, f32[2048]{0:T(1024)S(1)}, ...), condition=%wide.region_3.4_spmd.clone, body=%wide.region_0.3_spmd.clone.sunk | while | flops 554450944 | bytes 32435368 | solution.py:150
  197.8 3.7 %convolution_add_fusion.2 = f32[2048,128]{1,0:T(8,128)} fusion(f32[512,2048]{1,0:T(8,128)S(1)} %copy-done.1, f32[2048]{0:T(1024)S(1)} %ceil_maximum_fusion.2, s32[2048]{0:T(1024)S(1)} %ge.96, s32[512]{0:T(512)S(1)} %bitcast.144, f32[2048,128]{1,0:T(8,128)} %get-tuple-element.306, f32[2048]{0:T(1024)S(1)} %get-tuple-element.291, pred[]{:T(512)S(6)} %compare.3, ...), kind=kOutput, calls=%fused_computation.9.clone.1 | convolution fusion | flops 275513344 | bytes 6449157 | tf_op jit(solution)/shard_map/while/body/eval_jaxpr/dot_general | solution.py:97
  208.9 3.7 %convolution_add_fusion.2 = f32[2048,128]{1,0:T(8,128)} fusion(f32[512,2048]{1,0:T(8,128)S(1)} %copy-done.1, f32[2048]{0:T(1024)S(1)} %ceil_maximum_fusion.2, s32[2048]{0:T(1024)S(1)} %ge.96, s32[512]{0:T(512)S(1)} %bitcast.144, f32[2048,128]{1,0:T(8,128)} %get-tuple-element.306, f32[2048]{0:T(1024)S(1)} %get-tuple-element.291, pred[]{:T(512)S(6)} %compare.3, ...), kind=kOutput, calls=%fused_computation.9.clone.1 | convolution fusion | flops 275513344 | bytes 6449157 | tf_op jit(solution)/shard_map/while/body/eval_jaxpr/dot_general | solution.py:97
  219.9 3.7 %convolution_add_fusion.2 = f32[2048,128]{1,0:T(8,128)} fusion(f32[512,2048]{1,0:T(8,128)S(1)} %copy-done.1, f32[2048]{0:T(1024)S(1)} %ceil_maximum_fusion.2, s32[2048]{0:T(1024)S(1)} %ge.96, s32[512]{0:T(512)S(1)} %bitcast.144, f32[2048,128]{1,0:T(8,128)} %get-tuple-element.306, f32[2048]{0:T(1024)S(1)} %get-tuple-element.291, pred[]{:T(512)S(6)} %compare.3, ...), kind=kOutput, calls=%fused_computation.9.clone.1 | convolution fusion | flops 275513344 | bytes 6449157 | tf_op jit(solution)/shard_map/while/body/eval_jaxpr/dot_general | solution.py:97
  231.0 3.7 %convolution_add_fusion.2 = f32[2048,128]{1,0:T(8,128)} fusion(f32[512,2048]{1,0:T(8,128)S(1)} %copy-done.1, f32[2048]{0:T(1024)S(1)} %ceil_maximum_fusion.2, s32[2048]{0:T(1024)S(1)} %ge.96, s32[512]{0:T(512)S(1)} %bitcast.144, f32[2048,128]{1,0:T(8,128)} %get-tuple-element.306, f32[2048]{0:T(1024)S(1)} %get-tuple-element.291, pred[]{:T(512)S(6)} %compare.3, ...), kind=kOutput, calls=%fused_computation.9.clone.1 | convolution fusion | flops 275513344 | bytes 6449157 | tf_op jit(solution)/shard_map/while/body/eval_jaxpr/dot_general | solution.py:97
  242.0 3.7 %convolution_add_fusion.2 = f32[2048,128]{1,0:T(8,128)} fusion(f32[512,2048]{1,0:T(8,128)S(1)} %copy-done.1, f32[2048]{0:T(1024)S(1)} %ceil_maximum_fusion.2, s32[2048]{0:T(1024)S(1)} %ge.96, s32[512]{0:T(512)S(1)} %bitcast.144, f32[2048,128]{1,0:T(8,128)} %get-tuple-element.306, f32[2048]{0:T(1024)S(1)} %get-tuple-element.291, pred[]{:T(512)S(6)} %compare.3, ...), kind=kOutput, calls=%fused_computation.9.clone.1 | convolution fusion | flops 275513344 | bytes 6449157 | tf_op jit(solution)/shard_map/while/body/eval_jaxpr/dot_general | solution.py:97
  253.1 3.7 %convolution_add_fusion.2 = f32[2048,128]{1,0:T(8,128)} fusion(f32[512,2048]{1,0:T(8,128)S(1)} %copy-done.1, f32[2048]{0:T(1024)S(1)} %ceil_maximum_fusion.2, s32[2048]{0:T(1024)S(1)} %ge.96, s32[512]{0:T(512)S(1)} %bitcast.144, f32[2048,128]{1,0:T(8,128)} %get-tuple-element.306, f32[2048]{0:T(1024)S(1)} %get-tuple-element.291, pred[]{:T(512)S(6)} %compare.3, ...), kind=kOutput, calls=%fused_computation.9.clone.1 | convolution fusion | flops 275513344 | bytes 6449157 | tf_op jit(solution)/shard_map/while/body/eval_jaxpr/dot_general | solution.py:97
  264.1 3.7 %convolution_add_fusion.2 = f32[2048,128]{1,0:T(8,128)} fusion(f32[512,2048]{1,0:T(8,128)S(1)} %copy-done.1, f32[2048]{0:T(1024)S(1)} %ceil_maximum_fusion.2, s32[2048]{0:T(1024)S(1)} %ge.96, s32[512]{0:T(512)S(1)} %bitcast.144, f32[2048,128]{1,0:T(8,128)} %get-tuple-element.306, f32[2048]{0:T(1024)S(1)} %get-tuple-element.291, pred[]{:T(512)S(6)} %compare.3, ...), kind=kOutput, calls=%fused_computation.9.clone.1 | convolution fusion | flops 275513344 | bytes 6449157 | tf_op jit(solution)/shard_map/while/body/eval_jaxpr/dot_general | solution.py:97
  275.2 3.7 %convolution_add_fusion.2 = f32[2048,128]{1,0:T(8,128)} fusion(f32[512,2048]{1,0:T(8,128)S(1)} %copy-done.1, f32[2048]{0:T(1024)S(1)} %ceil_maximum_fusion.2, s32[2048]{0:T(1024)S(1)} %ge.96, s32[512]{0:T(512)S(1)} %bitcast.144, f32[2048,128]{1,0:T(8,128)} %get-tuple-element.306, f32[2048]{0:T(1024)S(1)} %get-tuple-element.291, pred[]{:T(512)S(6)} %compare.3, ...), kind=kOutput, calls=%fused_computation.9.clone.1 | convolution fusion | flops 275513344 | bytes 6449157 | tf_op jit(solution)/shard_map/while/body/eval_jaxpr/dot_general | solution.py:97
  286.2 3.7 %convolution_add_fusion.2 = f32[2048,128]{1,0:T(8,128)} fusion(f32[512,2048]{1,0:T(8,128)S(1)} %copy-done.1, f32[2048]{0:T(1024)S(1)} %ceil_maximum_fusion.2, s32[2048]{0:T(1024)S(1)} %ge.96, s32[512]{0:T(512)S(1)} %bitcast.144, f32[2048,128]{1,0:T(8,128)} %get-tuple-element.306, f32[2048]{0:T(1024)S(1)} %get-tuple-element.291, pred[]{:T(512)S(6)} %compare.3, ...), kind=kOutput, calls=%fused_computation.9.clone.1 | convolution fusion | flops 275513344 | bytes 6449157 | tf_op jit(solution)/shard_map/while/body/eval_jaxpr/dot_general | solution.py:97
  297.3 3.7 %convolution_add_fusion.2 = f32[2048,128]{1,0:T(8,128)} fusion(f32[512,2048]{1,0:T(8,128)S(1)} %copy-done.1, f32[2048]{0:T(1024)S(1)} %ceil_maximum_fusion.2, s32[2048]{0:T(1024)S(1)} %ge.96, s32[512]{0:T(512)S(1)} %bitcast.144, f32[2048,128]{1,0:T(8,128)} %get-tuple-element.306, f32[2048]{0:T(1024)S(1)} %get-tuple-element.291, pred[]{:T(512)S(6)} %compare.3, ...), kind=kOutput, calls=%fused_computation.9.clone.1 | convolution fusion | flops 275513344 | bytes 6449157 | tf_op jit(solution)/shard_map/while/body/eval_jaxpr/dot_general | solution.py:97
  308.3 3.7 %convolution_add_fusion.2 = f32[2048,128]{1,0:T(8,128)} fusion(f32[512,2048]{1,0:T(8,128)S(1)} %copy-done.1, f32[2048]{0:T(1024)S(1)} %ceil_maximum_fusion.2, s32[2048]{0:T(1024)S(1)} %ge.96, s32[512]{0:T(512)S(1)} %bitcast.144, f32[2048,128]{1,0:T(8,128)} %get-tuple-element.306, f32[2048]{0:T(1024)S(1)} %get-tuple-element.291, pred[]{:T(512)S(6)} %compare.3, ...), kind=kOutput, calls=%fused_computation.9.clone.1 | convolution fusion | flops 275513344 | bytes 6449157 | tf_op jit(solution)/shard_map/while/body/eval_jaxpr/dot_general | solution.py:97
  319.4 3.7 %convolution_add_fusion.2 = f32[2048,128]{1,0:T(8,128)} fusion(f32[512,2048]{1,0:T(8,128)S(1)} %copy-done.1, f32[2048]{0:T(1024)S(1)} %ceil_maximum_fusion.2, s32[2048]{0:T(1024)S(1)} %ge.96, s32[512]{0:T(512)S(1)} %bitcast.144, f32[2048,128]{1,0:T(8,128)} %get-tuple-element.306, f32[2048]{0:T(1024)S(1)} %get-tuple-element.291, pred[]{:T(512)S(6)} %compare.3, ...), kind=kOutput, calls=%fused_computation.9.clone.1 | convolution fusion | flops 275513344 | bytes 6449157 | tf_op jit(solution)/shard_map/while/body/eval_jaxpr/dot_general | solution.py:97
  330.4 3.7 %convolution_add_fusion.2 = f32[2048,128]{1,0:T(8,128)} fusion(f32[512,2048]{1,0:T(8,128)S(1)} %copy-done.1, f32[2048]{0:T(1024)S(1)} %ceil_maximum_fusion.2, s32[2048]{0:T(1024)S(1)} %ge.96, s32[512]{0:T(512)S(1)} %bitcast.144, f32[2048,128]{1,0:T(8,128)} %get-tuple-element.306, f32[2048]{0:T(1024)S(1)} %get-tuple-element.291, pred[]{:T(512)S(6)} %compare.3, ...), kind=kOutput, calls=%fused_computation.9.clone.1 | convolution fusion | flops 275513344 | bytes 6449157 | tf_op jit(solution)/shard_map/while/body/eval_jaxpr/dot_general | solution.py:97
  341.5 3.7 %convolution_add_fusion.2 = f32[2048,128]{1,0:T(8,128)} fusion(f32[512,2048]{1,0:T(8,128)S(1)} %copy-done.1, f32[2048]{0:T(1024)S(1)} %ceil_maximum_fusion.2, s32[2048]{0:T(1024)S(1)} %ge.96, s32[512]{0:T(512)S(1)} %bitcast.144, f32[2048,128]{1,0:T(8,128)} %get-tuple-element.306, f32[2048]{0:T(1024)S(1)} %get-tuple-element.291, pred[]{:T(512)S(6)} %compare.3, ...), kind=kOutput, calls=%fused_computation.9.clone.1 | convolution fusion | flops 275513344 | bytes 6449157 | tf_op jit(solution)/shard_map/while/body/eval_jaxpr/dot_general | solution.py:97
  (273 shorter events, 154.0 us)
Async XLA Ops:
  8.0 28.6 %copy-start = (bf16[256,8,128]{2,1,0:T(8,128)(2,1)S(1)}, bf16[256,8,128]{2,1,0:T(8,128)(2,1)}, u32[]{:S(2)}) copy-start(bf16[256,8,128]{2,1,0:T(8,128)(2,1)} %param.21) | copy-start | bytes 1572868
  37.9 15.8 %all-to-all-start.1 = ((f32[32,1,2048]{2,1,0:T(1,128)}), f32[32,1,2048]{2,1,0:T(1,128)S(1)}, u32[]{:S(2)}, u32[]{:S(2)}) async-start(f32[32,1,2048]{2,1,0:T(1,128)} %broadcast_in_dim.109), calls=%async_computation.1 | async-start | bytes 524288 | tf_op jit(solution)/shard_map/all_to_all | solution.py:54
  41.8 50.8 %reduce-scatter.4.cloned.1.call-start = ((), (), s32[]{:S(2)}) async-start(), calls=%async_computation.7 | async-start | bytes 1179648 | tf_op jit(solution)/shard_map/reduce_scatter | solution.py:67
  56.8 35.9 %copy-start.2 = (bf16[256,1,128]{2,0,1:T(8,128)(2,1)S(1)}, bf16[256,1,128]{2,0,1:T(8,128)(2,1)}, u32[]{:S(2)}) copy-start(bf16[256,1,128]{2,0,1:T(8,128)(2,1)} %param.17) | copy-start | bytes 196612
  56.8 35.9 %copy-start.3 = (bf16[256,1,128]{2,0,1:T(8,128)(2,1)S(1)}, bf16[256,1,128]{2,0,1:T(8,128)(2,1)}, u32[]{:S(2)}) copy-start(bf16[256,1,128]{2,0,1:T(8,128)(2,1)} %param.16) | copy-start | bytes 196612
  56.8 36.6 %copy-start.4 = (bf16[128,2,128]{2,1,0:T(2,128)(2,1)S(1)}, bf16[128,2,128]{2,1,0:T(2,128)(2,1)}, u32[]{:S(2)}) copy-start(bf16[128,2,128]{2,1,0:T(2,128)(2,1)} %param.23) | copy-start | bytes 196612
  56.8 36.6 %copy-start.5 = (bf16[128,2,128]{2,1,0:T(2,128)(2,1)S(1)}, bf16[128,2,128]{2,1,0:T(2,128)(2,1)}, u32[]{:S(2)}) copy-start(bf16[128,2,128]{2,1,0:T(2,128)(2,1)} %param.22) | copy-start | bytes 196612
  56.9 41.2 %copy-start.8 = (s32[256]{0:T(256)S(1)}, s32[256]{0:T(256)}, u32[]{:S(2)}) copy-start(s32[256]{0:T(256)} %param.24) | copy-start | bytes 3076
  58.4 94.8 %reduce-scatter.8.cloned.1.call-start = ((), (), s32[]{:S(2)}) async-start(), calls=%async_computation.9 | async-start | bytes 147456 | tf_op jit(solution)/shard_map/reduce_scatter | solution.py:67
  59.2 111.2 %reduce-scatter.6.cloned.1.call-start = ((), (), s32[]{:S(2)}) async-start(), calls=%async_computation.8 | async-start | bytes 163840 | tf_op jit(solution)/shard_map/reduce_scatter | solution.py:67
  92.7 84.2 %all-gather.3.cloned.1.call-start = ((), (), s32[]{:S(2)}) async-start(), calls=%async_computation.6 | async-start | bytes 4325376 | tf_op jit(solution)/shard_map/all_gather | solution.py:18
  94.2 52.0 %all-to-all-start.2 = ((bf16[128,2,256]{2,0,1:T(8,128)(2,1)}), bf16[128,2,256]{2,0,1:T(8,128)(2,1)S(1)}, u32[]{:S(2)}, u32[]{:S(2)}) async-start(bf16[128,2,256]{2,0,1:T(8,128)(2,1)} %pad_maximum_fusion.1), calls=%async_computation.4 | async-start | bytes 262144 | tf_op jit(solution)/shard_map/all_to_all | solution.py:45
  100.3 44.6 %copy-start.9 = (u32[256]{0:T(256)S(1)}, u32[256]{0:T(256)}, u32[]{:S(2)}) copy-start(u32[256]{0:T(256)} %constant.138) | copy-start | bytes 3076
  171.9 8.8 %copy-start.7 = (bf16[256,8,128]{2,1,0:T(8,128)(2,1)S(1)}, bf16[256,8,128]{2,1,0:T(8,128)(2,1)}, u32[]{:S(2)}) copy-start(bf16[256,8,128]{2,1,0:T(8,128)(2,1)} %param.15) | copy-start | bytes 1572868
  184.5 3.5 copy-start.1
  194.3 3.5 copy-start.1
  216.4 3.5 copy-start.1
  227.5 3.5 copy-start.1
  271.7 3.5 copy-start.1
  282.7 3.5 copy-start.1
  293.8 3.5 copy-start.1
  304.8 3.5 copy-start.1
  315.9 3.5 copy-start.1
  326.9 3.5 copy-start.1
  (7 other events, 23.3 us)
Sparse Core Ops, SparseCore 0:
  58.5 34.1 reduce-scatter.3
  95.1 35.5 reduce-scatter.7
  133.3 27.6 reduce-scatter.5
Sparse Core Ops, SparseCore 1:
  96.3 80.5 all-gather.2
where the time goes:
time: 367 us; the launch traced here: 366 us
  matrix products  122 us (33%)
  blocking collectives  80.6 us (22%)
  other arithmetic  69.4 us (19%)
  waiting for transfers between devices  50.3 us (14%)
  local copies, waits for them, and re-layouts  18.5 us (5%)
  between operations  16.4 us (4%)
  starting transfers between devices  7.94 us (2%)
    dot_general x16, matrix products, online_step(): jnp.dot(weights.astype(jnp.bfloat16), value_block, preferred_element_type...  58.4 us
    dot_general x16, matrix products, attend(): jnp.einsum('qd,kd->qk', query_rows, key_block, preferred_element_type=jnp...  57.2 us
    reduce_sum x16, other arithmetic, online_step(): new_mass = old_mass * factor + jnp.sum(weights, axis=1)  55.4 us
    all_gather x1, blocking collectives, body(): lax.all_gather(token_pos, CTX, axis=0, tiled=True)  42.4 us
    reduce_scatter x3, waiting for transfers between devices, summed_rows(): nearer = lax.psum_scatter(array, axes[0], scatter_dimension=dim, tiled=True)  33.4 us
    all_to_all x1, blocking collectives, sent_together(): lax.all_to_all(both, axis, split_axis=split_dim, concat_axis=concat_dim,...  21.9 us
    unnamed x1, blocking collectives  16.3 us
    all_to_all x1, waiting for transfers between devices, sent_to_all(): lax.all_to_all(jnp.broadcast_to(array[None], (devices, *array.shape)), ax...  11.8 us
  transfers between devices with their start and end apart: 6, of which 3 were waited for; matrix products, arithmetic and copies ran while one was open for 4% of the time, Pallas kernels for 0%

commit v1 on v0

--- a/solution.py
+++ b/solution.py
@@ -138,7 +138,9 @@
     running = start_state
     key_piece, value_piece, place_piece = (
         *side_by_side((local_keys, local_values), CTX, 0, 1),
-        lax.all_gather(token_pos, CTX, axis=0, tiled=True),
+        jnp.concatenate(
+            lax.all_to_all(jnp.stack([token_pos] * lax.axis_size(CTX)), CTX, 0, 0), axis=0
+        ),
     )
     row_count = key_piece.shape[0]
     block_rows = math.gcd(row_count, 512)

time: 367 us -> 367 us (level)
  blocking collectives: 80.6 us -> 39.6 us
  waiting for transfers between devices: 50.3 us -> 83.6 us
  starting transfers between devices: 7.94 us -> 15.1 us
    all_gather x1 -> x0, blocking collectives: 42.4 us -> none  [body(): lax.all_gather(token_pos, CTX, axis=0, tiled=True)]
    reduce_scatter x3, waiting for transfers between devices: 33.4 us -> 51.4 us  [summed_rows(): nearer = lax.psum_scatter(array, axes[0], scatter_dimension=dim, tiled=True)]
    all_gather x1, waiting for transfers between devices: 5.02 us -> 14.5 us  [side_by_side(): whole = lax.all_gather(both, axis, axis=dim, tiled=True)]
    all_to_all x0 -> x1, starting transfers between devices: none -> 7.16 us  [body(): lax.all_to_all(jnp.stack([token_pos] * lax.axis_size(CTX)), CTX, 0, 0)]
    all_to_all x0 -> x1, waiting for transfers between devices: none -> 5.69 us  [body(): lax.all_to_all(jnp.stack([token_pos] * lax.axis_size(CTX)), CTX, 0, 0)]
  transfers between devices with their start and end apart: 6 -> 7, of which waited for: 3 -> 7; matrix products, arithmetic and copies ran while one was open for 4% -> 5% of each run, Pallas kernels for 0% -> 0%
where the time goes in v1:
time: 367 us; the launch traced here: 366 us
  matrix products  122 us (33%)
  waiting for transfers between devices  83.6 us (23%)
  other arithmetic  69.4 us (19%)
  blocking collectives  39.6 us (11%)
  local copies, waits for them, and re-layouts  19.1 us (5%)
  between operations  16.4 us (4%)
  starting transfers between devices  15.1 us (4%)
    dot_general x16, matrix products, online_step(): jnp.dot(weights.astype(jnp.bfloat16), value_block, preferred_element_type...  58.4 us
    dot_general x16, matrix products, attend(): jnp.einsum('qd,kd->qk', query_rows, key_block, preferred_element_type=jnp...  57.2 us
    reduce_sum x16, other arithmetic, online_step(): new_mass = old_mass * factor + jnp.sum(weights, axis=1)  55.4 us
    reduce_scatter x3, waiting for transfers between devices, summed_rows(): nearer = lax.psum_scatter(array, axes[0], scatter_dimension=dim, tiled=True)  51.4 us
    all_to_all x1, blocking collectives, sent_together(): lax.all_to_all(both, axis, split_axis=split_dim, concat_axis=concat_dim,...  21.9 us
    unnamed x1, blocking collectives  17.6 us
    all_gather x1, waiting for transfers between devices, side_by_side(): whole = lax.all_gather(both, axis, axis=dim, tiled=True)  14.5 us
    all_to_all x1, waiting for transfers between devices, sent_to_all(): lax.all_to_all(jnp.broadcast_to(array[None], (devices, *array.shape)), ax...  11.8 us
  transfers between devices with their start and end apart: 7, of which 7 were waited for; matrix products, arithmetic and copies ran while one was open for 5% of the time, Pallas kernels for 0%

profile of v1, /device:TPU:8, one launch (start us, length us, event | category | flops | bytes accessed | tf_op | source)
XLA Modules:
  0.0 365.8 jit_solution(16928065230971751439)
XLA Ops:
  14.2 21.9 %all_to_all.42 = bf16[32,2,1025]{2,1,0:T(2,128)(2,1)S(1)} all-to-all(bf16[32,2,1025]{2,1,0:T(2,128)(2,1)S(1)} %reshape.284), channel_id=1, replica_groups=mesh['ctx_0'=8,'ctx_1'=4,'head'=4,'side'=2] {'ctx_0','ctx_1'}, dimensions={0} | all-to-all | bytes 262400 | tf_op jit(solution)/shard_map/all_to_all | solution.py:26
  37.9 3.9 %all-to-all-start.2 = ((f32[32,1,2048]{2,1,0:T(1,128)}), f32[32,1,2048]{2,1,0:T(1,128)S(1)}, u32[]{:S(2)}, u32[]{:S(2)}) async-start(f32[32,1,2048]{2,1,0:T(1,128)} %broadcast_in_dim.109), calls=%async_computation.2 | async-start | bytes 524288 | tf_op jit(solution)/shard_map/all_to_all | solution.py:54
  41.9 11.8 %all-to-all-done.2 = f32[32,1,2048]{2,1,0:T(1,128)S(1)} async-done(((f32[32,1,2048]{2,1,0:T(1,128)}), f32[32,1,2048]{2,1,0:T(1,128)S(1)}, u32[]{:S(2)}, u32[]{:S(2)}) %all-to-all-start.2) | async-done | bytes 262176 | tf_op jit(solution)/shard_map/all_to_all | solution.py:54
  59.3 33.5 %reduce-scatter.4.cloned.1.call-done = f32[32,8,128]{2,0,1:T(8,128)} async-done(((f32[256,8,128]{2,0,1:T(8,128)}), f32[32,8,128]{2,0,1:T(8,128)}) %reduce-scatter.4.cloned.1.call-update) | async-done | bytes 131088 | tf_op jit(solution)/shard_map/reduce_scatter | solution.py:67
  94.2 7.2 %all-to-all-start = ((s32[32,1,256]{2,1,0:T(1,128)}), s32[32,1,256]{2,1,0:T(1,128)S(1)}, u32[]{:S(2)}, u32[]{:S(2)}) async-start(s32[32,1,256]{2,1,0:T(1,128)} %stack.2), calls=%async_computation | async-start | bytes 65536 | tf_op jit(solution)/shard_map/all_to_all | solution.py:142
  105.5 5.7 %all-to-all-done = s32[32,1,256]{2,1,0:T(1,128)S(1)} async-done(((s32[32,1,256]{2,1,0:T(1,128)}), s32[32,1,256]{2,1,0:T(1,128)S(1)}, u32[]{:S(2)}, u32[]{:S(2)}) %all-to-all-start) | async-done | bytes 32800 | tf_op jit(solution)/shard_map/all_to_all | solution.py:142
  111.2 3.9 %all-to-all-start.3 = ((bf16[128,2,256]{2,0,1:T(8,128)(2,1)}), bf16[128,2,256]{2,0,1:T(8,128)(2,1)S(1)}, u32[]{:S(2)}, u32[]{:S(2)}) async-start(bf16[128,2,256]{2,0,1:T(8,128)(2,1)} %pad_maximum_fusion.1), calls=%async_computation.5 | async-start | bytes 262144 | tf_op jit(solution)/shard_map/all_to_all | solution.py:45
  124.5 6.3 %reduce-scatter.8.cloned.1.call-done = f32[32,8]{1,0:T(8,128)} async-done(((f32[256,8]{1,0:T(8,128)}), f32[32,8]{1,0:T(8,128)}) %reduce-scatter.8.cloned.1.call-update) | async-done | bytes 1040 | tf_op jit(solution)/shard_map/reduce_scatter | solution.py:67
  130.9 17.6 %all-reduce = f32[32,8]{1,0:T(8,128)S(1)} all-reduce(f32[32,8]{1,0:T(8,128)} %reduce-scatter.8.cloned.1.call-done), channel_id=5, replica_groups=mesh['ctx_0'=8,'ctx_1'=4,'head'=4,'side'=2] {'ctx_1'}, use_global_device_ids=true, to_apply=%region_13.15.clone | all-reduce | flops 256 | bytes 2048
  149.4 11.6 %reduce-scatter.6.cloned.1.call-done = f32[8,8,128]{2,0,1:T(8,128)} async-done(((f32[32,8,128]{2,0,1:T(8,128)}), f32[8,8,128]{2,0,1:T(8,128)}) %reduce-scatter.6.cloned.1.call-update) | async-done | bytes 32784 | tf_op jit(solution)/shard_map/reduce_scatter | solution.py:67
  162.5 14.5 %all-gather.2.cloned.1.call-done = bf16[8192,256]{1,0:T(8,128)(2,1)} async-done(((bf16[256,256]{1,0:T(8,128)(2,1)}), bf16[8192,256]{1,0:T(8,128)(2,1)}) %all-gather.2.cloned.1.call-update) | async-done | bytes 4194320 | tf_op jit(solution)/shard_map/all_gather | solution.py:18
  176.9 3.8 %fusion.54 = (bf16[8192,128]{1,0:T(8,128)(2,1)S(1)}, bf16[8192,128]{1,0:T(8,128)(2,1)}) fusion(bf16[8192,256]{1,0:T(8,128)(2,1)} %all-gather.2.cloned.1.call-done), kind=kLoop, calls=%fused_computation.116 | loop fusion | bytes 8388608 | tf_op jit(solution)/shard_map/split | solution.py:19
  180.7 175.6 %while.17 = (s32[]{:T(128)}, f32[2048]{0:T(1024)S(1)}, f32[2048]{0:T(1024)S(1)}, f32[2048,128]{1,0:T(8,128)}, s32[16,512]{1,0:T(8,128)S(1)}, /*index=5*/bf16[16,...) while((s32[]{:T(128)}, f32[2048]{0:T(1024)S(1)}, ...), condition=%wide.region_3.4_spmd.clone, body=%wide.region_0.3_spmd.clone.sunk | while | flops 554450944 | bytes 32435368 | solution.py:152
  197.9 3.7 %convolution_add_fusion.2 = f32[2048,128]{1,0:T(8,128)} fusion(f32[512,2048]{1,0:T(8,128)S(1)} %copy-done.1, f32[2048]{0:T(1024)S(1)} %ceil_maximum_fusion.2, s32[2048]{0:T(1024)S(1)} %ge.96, s32[512]{0:T(512)S(1)} %bitcast.143, f32[2048,128]{1,0:T(8,128)} %get-tuple-element.306, f32[2048]{0:T(1024)S(1)} %get-tuple-element.291, pred[]{:T(512)S(6)} %compare.3, ...), kind=kOutput, calls=%fused_computation.9.clone.1 | convolution fusion | flops 275513344 | bytes 6449157 | tf_op jit(solution)/shard_map/while/body/eval_jaxpr/dot_general | solution.py:97
  208.9 3.7 %convolution_add_fusion.2 = f32[2048,128]{1,0:T(8,128)} fusion(f32[512,2048]{1,0:T(8,128)S(1)} %copy-done.1, f32[2048]{0:T(1024)S(1)} %ceil_maximum_fusion.2, s32[2048]{0:T(1024)S(1)} %ge.96, s32[512]{0:T(512)S(1)} %bitcast.143, f32[2048,128]{1,0:T(8,128)} %get-tuple-element.306, f32[2048]{0:T(1024)S(1)} %get-tuple-element.291, pred[]{:T(512)S(6)} %compare.3, ...), kind=kOutput, calls=%fused_computation.9.clone.1 | convolution fusion | flops 275513344 | bytes 6449157 | tf_op jit(solution)/shard_map/while/body/eval_jaxpr/dot_general | solution.py:97
  220.0 3.7 %convolution_add_fusion.2 = f32[2048,128]{1,0:T(8,128)} fusion(f32[512,2048]{1,0:T(8,128)S(1)} %copy-done.1, f32[2048]{0:T(1024)S(1)} %ceil_maximum_fusion.2, s32[2048]{0:T(1024)S(1)} %ge.96, s32[512]{0:T(512)S(1)} %bitcast.143, f32[2048,128]{1,0:T(8,128)} %get-tuple-element.306, f32[2048]{0:T(1024)S(1)} %get-tuple-element.291, pred[]{:T(512)S(6)} %compare.3, ...), kind=kOutput, calls=%fused_computation.9.clone.1 | convolution fusion | flops 275513344 | bytes 6449157 | tf_op jit(solution)/shard_map/while/body/eval_jaxpr/dot_general | solution.py:97
  231.0 3.7 %convolution_add_fusion.2 = f32[2048,128]{1,0:T(8,128)} fusion(f32[512,2048]{1,0:T(8,128)S(1)} %copy-done.1, f32[2048]{0:T(1024)S(1)} %ceil_maximum_fusion.2, s32[2048]{0:T(1024)S(1)} %ge.96, s32[512]{0:T(512)S(1)} %bitcast.143, f32[2048,128]{1,0:T(8,128)} %get-tuple-element.306, f32[2048]{0:T(1024)S(1)} %get-tuple-element.291, pred[]{:T(512)S(6)} %compare.3, ...), kind=kOutput, calls=%fused_computation.9.clone.1 | convolution fusion | flops 275513344 | bytes 6449157 | tf_op jit(solution)/shard_map/while/body/eval_jaxpr/dot_general | solution.py:97
  242.1 3.7 %convolution_add_fusion.2 = f32[2048,128]{1,0:T(8,128)} fusion(f32[512,2048]{1,0:T(8,128)S(1)} %copy-done.1, f32[2048]{0:T(1024)S(1)} %ceil_maximum_fusion.2, s32[2048]{0:T(1024)S(1)} %ge.96, s32[512]{0:T(512)S(1)} %bitcast.143, f32[2048,128]{1,0:T(8,128)} %get-tuple-element.306, f32[2048]{0:T(1024)S(1)} %get-tuple-element.291, pred[]{:T(512)S(6)} %compare.3, ...), kind=kOutput, calls=%fused_computation.9.clone.1 | convolution fusion | flops 275513344 | bytes 6449157 | tf_op jit(solution)/shard_map/while/body/eval_jaxpr/dot_general | solution.py:97
  253.1 3.7 %convolution_add_fusion.2 = f32[2048,128]{1,0:T(8,128)} fusion(f32[512,2048]{1,0:T(8,128)S(1)} %copy-done.1, f32[2048]{0:T(1024)S(1)} %ceil_maximum_fusion.2, s32[2048]{0:T(1024)S(1)} %ge.96, s32[512]{0:T(512)S(1)} %bitcast.143, f32[2048,128]{1,0:T(8,128)} %get-tuple-element.306, f32[2048]{0:T(1024)S(1)} %get-tuple-element.291, pred[]{:T(512)S(6)} %compare.3, ...), kind=kOutput, calls=%fused_computation.9.clone.1 | convolution fusion | flops 275513344 | bytes 6449157 | tf_op jit(solution)/shard_map/while/body/eval_jaxpr/dot_general | solution.py:97
  308.4 3.7 %convolution_add_fusion.2 = f32[2048,128]{1,0:T(8,128)} fusion(f32[512,2048]{1,0:T(8,128)S(1)} %copy-done.1, f32[2048]{0:T(1024)S(1)} %ceil_maximum_fusion.2, s32[2048]{0:T(1024)S(1)} %ge.96, s32[512]{0:T(512)S(1)} %bitcast.143, f32[2048,128]{1,0:T(8,128)} %get-tuple-element.306, f32[2048]{0:T(1024)S(1)} %get-tuple-element.291, pred[]{:T(512)S(6)} %compare.3, ...), kind=kOutput, calls=%fused_computation.9.clone.1 | convolution fusion | flops 275513344 | bytes 6449157 | tf_op jit(solution)/shard_map/while/body/eval_jaxpr/dot_general | solution.py:97
  319.4 3.7 %convolution_add_fusion.2 = f32[2048,128]{1,0:T(8,128)} fusion(f32[512,2048]{1,0:T(8,128)S(1)} %copy-done.1, f32[2048]{0:T(1024)S(1)} %ceil_maximum_fusion.2, s32[2048]{0:T(1024)S(1)} %ge.96, s32[512]{0:T(512)S(1)} %bitcast.143, f32[2048,128]{1,0:T(8,128)} %get-tuple-element.306, f32[2048]{0:T(1024)S(1)} %get-tuple-element.291, pred[]{:T(512)S(6)} %compare.3, ...), kind=kOutput, calls=%fused_computation.9.clone.1 | convolution fusion | flops 275513344 | bytes 6449157 | tf_op jit(solution)/shard_map/while/body/eval_jaxpr/dot_general | solution.py:97
  330.5 3.7 %convolution_add_fusion.2 = f32[2048,128]{1,0:T(8,128)} fusion(f32[512,2048]{1,0:T(8,128)S(1)} %copy-done.1, f32[2048]{0:T(1024)S(1)} %ceil_maximum_fusion.2, s32[2048]{0:T(1024)S(1)} %ge.96, s32[512]{0:T(512)S(1)} %bitcast.143, f32[2048,128]{1,0:T(8,128)} %get-tuple-element.306, f32[2048]{0:T(1024)S(1)} %get-tuple-element.291, pred[]{:T(512)S(6)} %compare.3, ...), kind=kOutput, calls=%fused_computation.9.clone.1 | convolution fusion | flops 275513344 | bytes 6449157 | tf_op jit(solution)/shard_map/while/body/eval_jaxpr/dot_general | solution.py:97
  341.5 3.7 %convolution_add_fusion.2 = f32[2048,128]{1,0:T(8,128)} fusion(f32[512,2048]{1,0:T(8,128)S(1)} %copy-done.1, f32[2048]{0:T(1024)S(1)} %ceil_maximum_fusion.2, s32[2048]{0:T(1024)S(1)} %ge.96, s32[512]{0:T(512)S(1)} %bitcast.143, f32[2048,128]{1,0:T(8,128)} %get-tuple-element.306, f32[2048]{0:T(1024)S(1)} %get-tuple-element.291, pred[]{:T(512)S(6)} %compare.3, ...), kind=kOutput, calls=%fused_computation.9.clone.1 | convolution fusion | flops 275513344 | bytes 6449157 | tf_op jit(solution)/shard_map/while/body/eval_jaxpr/dot_general | solution.py:97
  352.6 3.7 %convolution_add_fusion.2 = f32[2048,128]{1,0:T(8,128)} fusion(f32[512,2048]{1,0:T(8,128)S(1)} %copy-done.1, f32[2048]{0:T(1024)S(1)} %ceil_maximum_fusion.2, s32[2048]{0:T(1024)S(1)} %ge.96, s32[512]{0:T(512)S(1)} %bitcast.143, f32[2048,128]{1,0:T(8,128)} %get-tuple-element.306, f32[2048]{0:T(1024)S(1)} %get-tuple-element.291, pred[]{:T(512)S(6)} %compare.3, ...), kind=kOutput, calls=%fused_computation.9.clone.1 | convolution fusion | flops 275513344 | bytes 6449157 | tf_op jit(solution)/shard_map/while/body/eval_jaxpr/dot_general | solution.py:97
  (275 shorter events, 166.0 us)
Async XLA Ops:
  8.0 28.6 %copy-start = (bf16[256,8,128]{2,1,0:T(8,128)(2,1)S(1)}, bf16[256,8,128]{2,1,0:T(8,128)(2,1)}, u32[]{:S(2)}) copy-start(bf16[256,8,128]{2,1,0:T(8,128)(2,1)} %param.21) | copy-start | bytes 1572868
  37.9 15.8 %all-to-all-start.2 = ((f32[32,1,2048]{2,1,0:T(1,128)}), f32[32,1,2048]{2,1,0:T(1,128)S(1)}, u32[]{:S(2)}, u32[]{:S(2)}) async-start(f32[32,1,2048]{2,1,0:T(1,128)} %broadcast_in_dim.109), calls=%async_computation.2 | async-start | bytes 524288 | tf_op jit(solution)/shard_map/all_to_all | solution.py:54
  41.8 50.9 %reduce-scatter.4.cloned.1.call-start = ((), (), s32[]{:S(2)}) async-start(), calls=%async_computation.8 | async-start | bytes 1179648 | tf_op jit(solution)/shard_map/reduce_scatter | solution.py:67
  56.8 36.0 %copy-start.2 = (bf16[256,1,128]{2,0,1:T(8,128)(2,1)S(1)}, bf16[256,1,128]{2,0,1:T(8,128)(2,1)}, u32[]{:S(2)}) copy-start(bf16[256,1,128]{2,0,1:T(8,128)(2,1)} %param.17) | copy-start | bytes 196612
  56.8 36.0 %copy-start.3 = (bf16[256,1,128]{2,0,1:T(8,128)(2,1)S(1)}, bf16[256,1,128]{2,0,1:T(8,128)(2,1)}, u32[]{:S(2)}) copy-start(bf16[256,1,128]{2,0,1:T(8,128)(2,1)} %param.16) | copy-start | bytes 196612
  56.8 36.7 %copy-start.6 = (s32[256]{0:T(256)S(1)}, s32[256]{0:T(256)}, u32[]{:S(2)}) copy-start(s32[256]{0:T(256)} %param.18) | copy-start | bytes 3076
  56.8 44.5 %copy-start.4 = (bf16[128,2,128]{2,1,0:T(2,128)(2,1)S(1)}, bf16[128,2,128]{2,1,0:T(2,128)(2,1)}, u32[]{:S(2)}) copy-start(bf16[128,2,128]{2,1,0:T(2,128)(2,1)} %param.23) | copy-start | bytes 196612
  56.9 44.5 %copy-start.5 = (bf16[128,2,128]{2,1,0:T(2,128)(2,1)S(1)}, bf16[128,2,128]{2,1,0:T(2,128)(2,1)}, u32[]{:S(2)}) copy-start(bf16[128,2,128]{2,1,0:T(2,128)(2,1)} %param.22) | copy-start | bytes 196612
  56.9 44.5 %copy-start.8 = (s32[256]{0:T(256)S(1)}, s32[256]{0:T(256)}, u32[]{:S(2)}) copy-start(s32[256]{0:T(256)} %param.24) | copy-start | bytes 3076
  58.4 72.5 %reduce-scatter.8.cloned.1.call-start = ((), (), s32[]{:S(2)}) async-start(), calls=%async_computation.10 | async-start | bytes 147456 | tf_op jit(solution)/shard_map/reduce_scatter | solution.py:67
  59.2 101.8 %reduce-scatter.6.cloned.1.call-start = ((), (), s32[]{:S(2)}) async-start(), calls=%async_computation.9 | async-start | bytes 163840 | tf_op jit(solution)/shard_map/reduce_scatter | solution.py:67
  92.7 84.2 %all-gather.2.cloned.1.call-start = ((), (), s32[]{:S(2)}) async-start(), calls=%async_computation.7 | async-start | bytes 4325376 | tf_op jit(solution)/shard_map/all_gather | solution.py:18
  94.2 17.0 %all-to-all-start = ((s32[32,1,256]{2,1,0:T(1,128)}), s32[32,1,256]{2,1,0:T(1,128)S(1)}, u32[]{:S(2)}, u32[]{:S(2)}) async-start(s32[32,1,256]{2,1,0:T(1,128)} %stack.2), calls=%async_computation | async-start | bytes 65536 | tf_op jit(solution)/shard_map/all_to_all | solution.py:142
  103.6 12.4 %copy-start.9 = (u32[256]{0:T(256)S(1)}, u32[256]{0:T(256)}, u32[]{:S(2)}) copy-start(u32[256]{0:T(256)} %constant.138) | copy-start | bytes 3076
  111.2 6.4 %all-to-all-start.3 = ((bf16[128,2,256]{2,0,1:T(8,128)(2,1)}), bf16[128,2,256]{2,0,1:T(8,128)(2,1)S(1)}, u32[]{:S(2)}, u32[]{:S(2)}) async-start(bf16[128,2,256]{2,0,1:T(8,128)(2,1)} %pad_maximum_fusion.1), calls=%async_computation.5 | async-start | bytes 262144 | tf_op jit(solution)/shard_map/all_to_all | solution.py:45
  162.5 18.3 %copy-start.7 = (bf16[256,8,128]{2,1,0:T(8,128)(2,1)S(1)}, bf16[256,8,128]{2,1,0:T(8,128)(2,1)}, u32[]{:S(2)}) copy-start(bf16[256,8,128]{2,1,0:T(8,128)(2,1)} %param.15) | copy-start | bytes 1572868
  184.6 3.5 copy-start.1
  205.4 3.5 copy-start.1
  216.5 3.5 copy-start.1
  227.5 3.5 copy-start.1
  238.6 3.5 copy-start.1
  249.6 3.5 copy-start.1
  260.7 3.5 copy-start.1
  271.7 3.5 copy-start.1
  (8 other events, 28.0 us)
Sparse Core Ops, SparseCore 0:
  58.5 34.1 reduce-scatter.3
  95.2 35.5 reduce-scatter.7
  133.4 27.5 reduce-scatter.5
Sparse Core Ops, SparseCore 1:
  96.4 80.5 all-gather.1
